TPU v7x, 256 devices: a whole 4x4x8 slice. The times are simulated.
256 devices in a mesh: dp: 64 (over y, z, core), tensor: 4 (over x).
Axes of the slice: x: 4, y: 4, z: 8, core: 2. Of those that a mesh axis runs over, the one named last changes fastest.
Arguments:
- hidden: bfloat16 [1024, 4096], P(('dp', 'tensor')), may hold values from -6 to 6
- shortcut: bfloat16 [1024, 4096], P('dp'), may hold values from -6 to 6
- expert_ids: int32 [1024, 2], P('dp'), may hold values from 0 to 7, all different within a row; in each aligned block of 16 rows (0 to 15, 16 to 31, ...) at most 6 rows name the same one
- route_weight: float32 [1024, 2], P('dp'), may hold values from 0.1 to 1
- dense_gain: float32 [4096], replicated, may hold values from 0.5 to 1.5
- moe_gain: float32 [4096], replicated, may hold values from 0.5 to 1.5
- dense_gate: bfloat16 [4096, 8192], P(None, 'dp'), may hold values from -0.09375 to 0.09375
- dense_lift: bfloat16 [4096, 8192], P(None, 'dp'), may hold values from -0.09375 to 0.09375
- dense_down: bfloat16 [8192, 4096], P('dp'), may hold values from -0.0625 to 0.0625
- expert_gate: bfloat16 [4096, 65536], P(None, ('dp', 'tensor')), may hold values from -0.09375 to 0.09375
- expert_lift: bfloat16 [4096, 65536], P(None, ('dp', 'tensor')), may hold values from -0.09375 to 0.09375
- expert_down: bfloat16 [65536, 4096], P(('dp', 'tensor')), may hold values from -0.0625 to 0.0625
Outputs:
- mixed: bfloat16 [1024, 4096], P(('dp', 'tensor'))
Inputs may be any that keep to these rules, and one draw needn't show every extreme that they name: `expert_ids`: the 2 experts of a token differ. In each aligned block of 16 rows (the tokens of one index of dp) no expert is named by more than 6 rows, and in every draw some expert is named by exactly 6 rows of some block; every expert is named somewhere.
All inputs are finite; a program needn't handle non-finite values.
Results may differ from a plain program's by a relative error of at most 0.006.
Values may be sent and summed in bfloat16 or wider, within the bound.
No kernel may reach another device: no remote copies, remote signals or barrier semaphores. Data moves between devices by JAX's collectives and lax.ppermute only.
A program may use at most 64 MiB of HBM per device.

v0:
```python
import jax
import jax.numpy as jnp
from jax import lax
from jax.sharding import PartitionSpec as P

D = 4096
E = 8
TOP = 2
CAP = 6
EPSILON = 1e-05


def cut_along(value, dim, devices):
    lengths = value.shape
    parts = value.reshape(*lengths[:dim], devices, lengths[dim] // devices, *lengths[dim + 1 :])
    return jnp.moveaxis(parts, dim, 0)


def summed_on_arrival(value, axis, dim):
    devices = lax.axis_size(axis)
    parts = lax.all_to_all(cut_along(value, dim, devices), axis, 0, 0, tiled=True)
    return jnp.sum(parts.astype(jnp.float32), axis=0)


def sent_and_summed(value, axis, dim):
    parts = cut_along(value, dim, lax.axis_size(axis))
    arrived = lax.all_to_all(parts, axis, split_axis=0, concat_axis=0, tiled=True)
    return arrived.sum(axis=0)


def normalize(values_in, gain):
    values = values_in.astype(jnp.float32)
    scale = lax.rsqrt(jnp.mean(values * values, axis=-1, keepdims=True) + EPSILON)
    return (values * scale * gain).astype(jnp.bfloat16)


def local(
    hidden,
    shortcut,
    expert_ids,
    route_weight,
    dense_gain,
    moe_gain,
    dense_gate,
    dense_lift,
    dense_down,
    expert_gate,
    expert_lift,
    expert_down,
):
    normed = normalize(hidden, dense_gain)
    piece = lax.all_gather(normed, "dp", axis=0, tiled=True)
    gate_vals = jnp.dot(piece, dense_gate, preferred_element_type=jnp.float32)
    lift_vals = jnp.dot(piece, dense_lift, preferred_element_type=jnp.float32)
    dense_inner = (jax.nn.silu(gate_vals) * lift_vals).astype(jnp.bfloat16)
    dense_out = summed_on_arrival(
        jnp.dot(dense_inner, dense_down, preferred_element_type=jnp.float32).astype(jnp.bfloat16),
        "dp",
        0,
    )
    members = lax.axis_size("dp") // E
    token_count = shortcut.shape[0]
    moe_in = normalize(shortcut, moe_gain)
    flat = expert_ids.reshape(token_count * TOP)
    picked = (flat[:, None] == jnp.arange(E, dtype=jnp.int32)[None, :]).astype(jnp.int32)
    before = jnp.cumsum(picked, axis=0) - picked
    places = flat * CAP + jnp.sum(before * picked, axis=1)
    chosen = (places[:, None] == jnp.arange(E * CAP, dtype=jnp.int32)[None, :]).astype(jnp.float32)
    chosen = chosen.reshape(token_count, TOP, E * CAP)
    spread = jnp.sum(chosen, axis=1).astype(jnp.bfloat16)
    weighted = jnp.sum(chosen * route_weight[:, :, None], axis=1)
    buffer = lax.dot_general(
        spread, moe_in, (((0,), (0,)), ((), ())), preferred_element_type=jnp.float32
    )
    buffer = buffer.astype(jnp.bfloat16).reshape(E, CAP, D)
    outgoing = jnp.repeat(buffer, members, axis=0)
    arrived = lax.all_to_all(outgoing, "dp", split_axis=0, concat_axis=0, tiled=True)
    sources, count, width = arrived.shape
    rows_in = arrived.reshape(sources * count, width)
    gate_vals = jnp.dot(rows_in, expert_gate, preferred_element_type=jnp.float32)
    lift_vals = jnp.dot(rows_in, expert_lift, preferred_element_type=jnp.float32)
    inner = (jax.nn.silu(gate_vals) * lift_vals).astype(jnp.bfloat16)
    terms = jnp.dot(inner, expert_down, preferred_element_type=jnp.float32).astype(jnp.bfloat16)
    returned = lax.all_to_all(
        terms.reshape(sources, count, D), "dp", split_axis=0, concat_axis=0, tiled=True
    )
    summed = jnp.sum(returned.astype(jnp.float32).reshape(E, members, CAP, D), axis=1).reshape(
        E * CAP, D
    )
    moe_part = jnp.dot(
        weighted, summed, precision=lax.Precision.HIGHEST, preferred_element_type=jnp.float32
    )
    moe_out = sent_and_summed(moe_part, "tensor", 0)
    return (hidden.astype(jnp.float32) + dense_out + moe_out).astype(jnp.bfloat16)


def solution(mesh):
    in_specs = (
        P(("dp", "tensor"), None),
        P("dp", None),
        P("dp", None),
        P("dp", None),
        P(),
        P(),
        P(None, "dp"),
        P(None, "dp"),
        P("dp", None),
        P(None, ("dp", "tensor")),
        P(None, ("dp", "tensor")),
        P(("dp", "tensor"), None),
    )
    out_specs = P(("dp", "tensor"), None)
    return jax.shard_map(local, mesh=mesh, in_specs=in_specs, out_specs=out_specs, check_vma=False)
```

profile of v0, /device:TPU:1, one launch (start us, length us, event | category | flops | bytes accessed | tf_op | source)
XLA Modules:
  0.0 332.7 jit_solution(13501166355664263416)
XLA Ops:
  6.5 0.9 copy.29
  8.7 1.0 fusion.7
  9.8 0.8 convert_reduce_fusion.2
  10.5 1.2 convolution_convert_fusion.2
  12.4 109.2 %all_to_all.20 = bf16[64,6,4096]{2,1,0:T(8,128)(2,1)} all-to-all(bf16[64,6,4096]{2,1,0:T(8,128)(2,1)S(1)} %bitcast.20), channel_id=1, replica_groups=mesh['dp'=64,'tensor'=4] {'dp'}, dimensions={0} | all-to-all | bytes 6291456 | tf_op jit(solution)/shard_map/all_to_all | solution.py:77
  121.6 5.7 %reshape.67 = bf16[384,4096]{1,0:T(8,128)(2,1)} reshape(bf16[64,6,4096]{2,1,0:T(8,128)(2,1)} %all_to_all.20) | data formatting | bytes 6291456 | tf_op jit(solution)/shard_map/reshape | solution.py:79
  127.3 3.5 %fusion.31 = f32[384,256]{1,0:T(8,128)S(1)} fusion(bf16[384,4096]{1,0:T(8,128)(2,1)} %reshape.67, bf16[4096,256]{1,0:T(8,128)(2,1)} %param.21), kind=kOutput, calls=%fused_computation.50 | convolution fusion | flops 805306368 | bytes 5636096 | tf_op jit(solution)/shard_map/dot_general | solution.py:80
  130.9 7.6 %convolution_convert_fusion = bf16[384,4096]{1,0:T(8,128)(2,1)} fusion(bf16[256,4096]{1,0:T(8,128)(2,1)S(1)} %copy-done, bf16[384,4096]{1,0:T(8,128)(2,1)} %reshape.67, bf16[4096,256]{1,0:T(8,128)(2,1)} %param.22, f32[384,256]{1,0:T(8,128)S(1)} %fusion.31), kind=kOutput, calls=%fused_computation.1 | convolution fusion | flops 1612775424 | bytes 10878976 | tf_op jit(solution)/shard_map/dot_general | solution.py:83
  138.5 5.6 %reshape.68 = bf16[64,6,4096]{2,1,0:T(8,128)(2,1)} reshape(bf16[384,4096]{1,0:T(8,128)(2,1)} %convolution_convert_fusion) | data formatting | bytes 6291456 | tf_op jit(solution)/shard_map/reshape | solution.py:85
  144.2 6.2 %all-to-all-start.2 = ((bf16[64,6,4096]{2,1,0:T(8,128)(2,1)}), bf16[64,6,4096]{2,1,0:T(8,128)(2,1)}, u32[]{:S(2)}, u32[]{:S(2)}) async-start(bf16[64,6,4096]{2,1,0:T(8,128)(2,1)} %reshape.68), calls=%async_computation.2 | async-start | bytes 8388608 | tf_op jit(solution)/shard_map/all_to_all | solution.py:84
  150.5 0.7 fusion.25
  151.3 90.5 %all-gather.3.cloned.1.call-done = bf16[64,4,4096]{2,1,0:T(4,128)(2,1)} async-done(((bf16[1,4,4096]{2,1,0:T(4,128)(2,1)}), bf16[64,4,4096]{2,1,0:T(4,128)(2,1)}) %all-gather.3.cloned.1.call-update) | async-done | bytes 2097168 | tf_op jit(solution)/shard_map/all_gather | solution.py:52
  241.7 4.0 %reshape.75 = bf16[256,4096]{1,0:T(8,128)(2,1)} reshape(bf16[64,4,4096]{2,1,0:T(4,128)(2,1)} %all-gather.3.cloned.1.call-done) | data formatting | bytes 4194304
  245.7 2.3 fusion.30
  248.0 4.8 %convolution_convert_fusion.1 = bf16[256,4096]{1,0:T(8,128)(2,1)} fusion(bf16[128,4096]{1,0:T(8,128)(2,1)} %param.20, bf16[256,4096]{1,0:T(8,128)(2,1)} %reshape.75, bf16[4096,128]{1,0:T(8,128)(2,1)} %param.19, f32[256,128]{1,0:T(8,128)S(1)} %fusion.30), kind=kOutput, calls=%fused_computation.2 | convolution fusion | flops 538116096 | bytes 6422528 | tf_op jit(solution)/shard_map/dot_general | solution.py:57
  252.8 4.1 %reshape.64 = bf16[64,4,4096]{2,1,0:T(4,128)(2,1)} reshape(bf16[256,4096]{1,0:T(8,128)(2,1)} %convolution_convert_fusion.1) | data formatting | bytes 4194304 | tf_op jit(solution)/shard_map/reshape | solution.py:15
  257.0 7.4 %all-to-all-start = ((bf16[64,4,4096]{2,1,0:T(4,128)(2,1)}), bf16[64,4,4096]{2,1,0:T(4,128)(2,1)}, u32[]{:S(2)}, u32[]{:S(2)}) async-start(bf16[64,4,4096]{2,1,0:T(4,128)(2,1)} %reshape.64), calls=%async_computation | async-start | bytes 4194304 | tf_op jit(solution)/shard_map/all_to_all | solution.py:21
  264.4 3.3 convert_reduce_fusion
  267.6 1.0 reshape.76
  268.6 2.4 fusion.32
  271.0 44.5 %all-to-all-done = bf16[64,4,4096]{2,1,0:T(4,128)(2,1)} async-done(((bf16[64,4,4096]{2,1,0:T(4,128)(2,1)}), bf16[64,4,4096]{2,1,0:T(4,128)(2,1)}, u32[]{:S(2)}, u32[]{:S(2)}) %all-to-all-start) | async-done | bytes 2097184 | tf_op jit(solution)/shard_map/all_to_all | solution.py:21
  315.5 3.9 %all-to-all-start.3 = ((f32[4,4,4096]{2,1,0:T(4,128)}), f32[4,4,4096]{2,1,0:T(4,128)S(1)}, u32[]{:S(2)}, u32[]{:S(2)}) async-start(f32[4,4,4096]{2,1,0:T(4,128)} %fusion.32), calls=%async_computation.3 | async-start | bytes 524288 | tf_op jit(solution)/shard_map/all_to_all | solution.py:27
  319.4 2.4 convert_reduce_fusion.1
  321.8 3.3 %all-to-all-done.3 = f32[4,4,4096]{2,1,0:T(4,128)S(1)} async-done(((f32[4,4,4096]{2,1,0:T(4,128)}), f32[4,4,4096]{2,1,0:T(4,128)S(1)}, u32[]{:S(2)}, u32[]{:S(2)}) %all-to-all-start.3) | async-done | bytes 262176 | tf_op jit(solution)/shard_map/all_to_all | solution.py:27
  (25 shorter events, 2.8 us)
Async XLA Ops:
  6.5 124.3 %copy-start = (bf16[256,4096]{1,0:T(8,128)(2,1)S(1)}, bf16[256,4096]{1,0:T(8,128)(2,1)}, u32[]{:S(2)}) copy-start(bf16[256,4096]{1,0:T(8,128)(2,1)} %param.23) | copy-start | bytes 6291460
  144.2 6.2 %copy-start.2 = (bf16[4,4096]{1,0:T(4,128)(2,1)S(1)}, bf16[4,4096]{1,0:T(4,128)(2,1)}, u32[]{:S(2)}) copy-start(bf16[4,4096]{1,0:T(4,128)(2,1)} %param.12) | copy-start | bytes 98308
  144.2 6.4 %copy-start.3 = (f32[4096]{0:T(1024)S(1)}, f32[4096]{0:T(1024)}, u32[]{:S(2)}) copy-start(f32[4096]{0:T(1024)} %param.16) | copy-start | bytes 49156
  144.2 112.8 %all-to-all-start.2 = ((bf16[64,6,4096]{2,1,0:T(8,128)(2,1)}), bf16[64,6,4096]{2,1,0:T(8,128)(2,1)}, u32[]{:S(2)}, u32[]{:S(2)}) async-start(bf16[64,6,4096]{2,1,0:T(8,128)(2,1)} %reshape.68), calls=%async_computation.2 | async-start | bytes 8388608 | tf_op jit(solution)/shard_map/all_to_all | solution.py:84
  150.3 91.4 %all-gather.3.cloned.1.call-start = ((), (), s32[]{:S(2)}) async-start(), calls=%async_computation.4 | async-start | bytes 2129920 | tf_op jit(solution)/shard_map/all_gather | solution.py:52
  151.3 94.5 %copy-start.1 = (bf16[4096,128]{1,0:T(8,128)(2,1)S(1)}, bf16[4096,128]{1,0:T(8,128)(2,1)}, u32[]{:S(2)}) copy-start(bf16[4096,128]{1,0:T(8,128)(2,1)} %param.18) | copy-start | bytes 3145732
  257.0 58.5 %all-to-all-start = ((bf16[64,4,4096]{2,1,0:T(4,128)(2,1)}), bf16[64,4,4096]{2,1,0:T(4,128)(2,1)}, u32[]{:S(2)}, u32[]{:S(2)}) async-start(bf16[64,4,4096]{2,1,0:T(4,128)(2,1)} %reshape.64), calls=%async_computation | async-start | bytes 4194304 | tf_op jit(solution)/shard_map/all_to_all | solution.py:21
  315.5 9.7 %all-to-all-start.3 = ((f32[4,4,4096]{2,1,0:T(4,128)}), f32[4,4,4096]{2,1,0:T(4,128)S(1)}, u32[]{:S(2)}, u32[]{:S(2)}) async-start(f32[4,4,4096]{2,1,0:T(4,128)} %fusion.32), calls=%async_computation.3 | async-start | bytes 524288 | tf_op jit(solution)/shard_map/all_to_all | solution.py:27
Sparse Core Ops, SparseCore 0:
  153.9 87.7 all-gather.2
where the time goes:
time: 334 us; the launch traced here: 333 us
  waiting for transfers between devices  138 us (41%)
  blocking collectives  109 us (33%)
  local copies, waits for them, and re-layouts  22.3 us (7%)
  matrix products  21.8 us (7%)
  starting transfers between devices  17.5 us (5%)
  between operations  13.5 us (4%)
  other arithmetic  10.1 us (3%)
    all_to_all x1, blocking collectives, local(): lax.all_to_all(outgoing, 'dp', split_axis=0, concat_axis=0, tiled=True)  109 us
    all_gather x1, waiting for transfers between devices, local(): piece = lax.all_gather(normed, 'dp', axis=0, tiled=True)  90.5 us
    all_to_all x1, waiting for transfers between devices, summed_on_arrival(): lax.all_to_all(cut_along(value, dim, devices), axis, 0, 0, tiled=True)  44.5 us
    dot_general x1, matrix products, local(): jnp.dot(inner, expert_down, preferred_element_type=jnp.float32)  7.64 us
    all_to_all x1, starting transfers between devices, summed_on_arrival(): lax.all_to_all(cut_along(value, dim, devices), axis, 0, 0, tiled=True)  7.4 us
  transfers between devices with their start and end apart: 4, of which 3 were waited for; matrix products, arithmetic and copies ran while one was open for 8% of the time, Pallas kernels for 0%

commit v1 on v0

--- a/solution.py
+++ b/solution.py
@@ -8,6 +8,24 @@
 TOP = 2
 CAP = 6
 EPSILON = 1e-05
+
+
+def laid_out(blocks, dim):
+    blocks = jnp.moveaxis(blocks, 0, dim)
+    lengths = blocks.shape
+    return blocks.reshape(*lengths[:dim], lengths[dim] * lengths[dim + 1], *lengths[dim + 2 :])
+
+
+def collected_by_bits(x, axis):
+    peers = lax.axis_size(axis)
+    blocks = x[None]
+    for level in range(peers.bit_length() - 1):
+        distance = 1 << level
+        theirs = lax.ppermute(blocks, axis, [(i, i ^ distance) for i in range(peers)])
+        both = jnp.stack([blocks, theirs])
+        upper = lax.axis_index(axis) >> level & 1
+        blocks = jnp.where(upper == 0, both, both[::-1]).reshape(-1, *x.shape)
+    return blocks
 
 
 def cut_along(value, dim, devices):
@@ -49,7 +67,7 @@
     expert_down,
 ):
     normed = normalize(hidden, dense_gain)
-    piece = lax.all_gather(normed, "dp", axis=0, tiled=True)
+    piece = laid_out(collected_by_bits(normed, "dp"), 0)
     gate_vals = jnp.dot(piece, dense_gate, preferred_element_type=jnp.float32)
     lift_vals = jnp.dot(piece, dense_lift, preferred_element_type=jnp.float32)
     dense_inner = (jax.nn.silu(gate_vals) * lift_vals).astype(jnp.bfloat16)

time: 334 us -> 340 us (1.018)
  blocking collectives: 109 us -> 0 us
  waiting for transfers between devices: 138 us -> 219 us
  starting transfers between devices: 17.5 us -> 56.5 us
  between operations: 13.5 us -> 0.2 us
  other arithmetic: 10.1 us -> 17 us
    ppermute x0 -> x6, waiting for transfers between devices: none -> 171 us  [collected_by_bits(): lax.ppermute(blocks, axis, [(i, i ^ distance) for i in range(peers)])]
    all_to_all x1 -> x0, blocking collectives: 109 us -> none  [local(): lax.all_to_all(outgoing, 'dp', split_axis=0, concat_axis=0, tiled=True)]
    all_gather x1 -> x0, waiting for transfers between devices: 90.5 us -> none  [local(): piece = lax.all_gather(normed, 'dp', axis=0, tiled=True)]
    all_to_all x1, starting transfers between devices: 7.4 us -> 21.2 us  [summed_on_arrival(): lax.all_to_all(cut_along(value, dim, devices), axis, 0, 0, tiled=True)]
    all_to_all x0 -> x1, starting transfers between devices: none -> 13.5 us  [local(): lax.all_to_all(outgoing, 'dp', split_axis=0, concat_axis=0, tiled=True)]
    ppermute x0 -> x6, starting transfers between devices: none -> 11 us  [collected_by_bits(): lax.ppermute(blocks, axis, [(i, i ^ distance) for i in range(peers)])]
    another operation x0 -> x8, other arithmetic: none -> 4.36 us  [collected_by_bits(): both = jnp.stack([blocks, theirs])]
    another operation x0 -> x1, local copies, waits for them, and re-layouts: none -> 4.09 us  [laid_out(): blocks.reshape(*lengths[:dim], lengths[dim] * lengths[dim + 1], *lengths[...]
  transfers between devices with their start and end apart: 4 -> 10, of which waited for: 3 -> 7; matrix products, arithmetic and copies ran while one was open for 8% -> 16% of each run, Pallas kernels for 0% -> 0%
where the time goes in v1:
time: 340 us; the launch traced here: 339 us
  waiting for transfers between devices  219 us (64%)
  starting transfers between devices  56.5 us (17%)
  local copies, waits for them, and re-layouts  24.4 us (7%)
  matrix products  21.8 us (6%)
  other arithmetic  17 us (5%)
    ppermute x6, waiting for transfers between devices, collected_by_bits(): lax.ppermute(blocks, axis, [(i, i ^ distance) for i in range(peers)])  171 us
    all_to_all x1, waiting for transfers between devices, summed_on_arrival(): lax.all_to_all(cut_along(value, dim, devices), axis, 0, 0, tiled=True)  44.5 us
    all_to_all x1, starting transfers between devices, summed_on_arrival(): lax.all_to_all(cut_along(value, dim, devices), axis, 0, 0, tiled=True)  21.2 us
    all_to_all x1, starting transfers between devices, local(): lax.all_to_all(outgoing, 'dp', split_axis=0, concat_axis=0, tiled=True)  13.5 us
    ppermute x6, starting transfers between devices, collected_by_bits(): lax.ppermute(blocks, axis, [(i, i ^ distance) for i in range(peers)])  11 us
    dot_general x1, matrix products, local(): jnp.dot(inner, expert_down, preferred_element_type=jnp.float32)  7.64 us
  transfers between devices with their start and end apart: 10, of which 7 were waited for; matrix products, arithmetic and copies ran while one was open for 16% of the time, Pallas kernels for 0%

profile of v1, /device:TPU:1, one launch (start us, length us, event | category | flops | bytes accessed | tf_op | source)
XLA Modules:
  0.0 338.6 jit_solution(5690022049367147002)
XLA Ops:
  5.4 2.5 broadcast_in_dim.5
  7.9 13.5 %all-to-all-start.1 = ((bf16[64,6,4096]{2,1,0:T(8,128)(2,1)}), bf16[64,6,4096]{2,1,0:T(8,128)(2,1)}, u32[]{:S(2)}, u32[]{:S(2)}) async-start(bf16[64,6,4096]{2,1,0:T(8,128)(2,1)} %bitcast.40), calls=%async_computation.1 | async-start | bytes 8388608 | tf_op jit(solution)/shard_map/all_to_all | solution.py:95
  24.5 89.9 %collective-permute-done.1 = bf16[2,4,4096]{2,1,0:T(4,128)(2,1)S(1)} collective-permute-done((bf16[2,4,4096]{2,1,0:T(4,128)(2,1)S(1)}, bf16[2,4,4096]{2,1,0:T(4,128)(2,1)S(1)}, u32[]{:S(2)}, u32[]{:S(2)}) %collective-permute-start.1) | collective-permute-done | bytes 65568 | tf_op jit(solution)/shard_map/ppermute | solution.py:24
  115.0 8.7 %collective-permute-done.2 = bf16[4,4,4096]{2,1,0:T(4,128)(2,1)S(1)} collective-permute-done((bf16[4,4,4096]{2,1,0:T(4,128)(2,1)S(1)}, bf16[4,4,4096]{2,1,0:T(4,128)(2,1)S(1)}, u32[]{:S(2)}, u32[]{:S(2)}) %collective-permute-start.2) | collective-permute-done | bytes 131104 | tf_op jit(solution)/shard_map/ppermute | solution.py:24
  124.0 4.3 %collective-permute-start.3 = (bf16[8,4,4096]{2,1,0:T(4,128)(2,1)S(1)}, bf16[8,4,4096]{2,1,0:T(4,128)(2,1)S(1)}, u32[]{:S(2)}, u32[]{:S(2)}) collective-permute-start(bf16[8,4,4096]{2,1,0:T(4,128)(2,1)S(1)} %bitcast.45), channel_id=1, source_target_pairs={{0,32},{4,36},{8,40},{12,44},{16,48},{20,52},{24,56},{28,60},{32,0... | collective-permute-start | bytes 786440 | tf_op jit(solution)/shard_map/ppermute | solution.py:24
  128.3 5.7 %reshape.87 = bf16[384,4096]{1,0:T(8,128)(2,1)} reshape(bf16[64,6,4096]{2,1,0:T(8,128)(2,1)} %all-to-all-done.1) | data formatting | bytes 6291456 | tf_op jit(solution)/shard_map/reshape | solution.py:97
  134.0 3.5 %fusion.34 = f32[384,256]{1,0:T(8,128)S(1)} fusion(bf16[384,4096]{1,0:T(8,128)(2,1)} %reshape.87, bf16[4096,256]{1,0:T(8,128)(2,1)} %param.21), kind=kOutput, calls=%fused_computation.65 | convolution fusion | flops 805306368 | bytes 5636096 | tf_op jit(solution)/shard_map/dot_general | solution.py:98
  137.6 7.6 %convolution_convert_fusion = bf16[384,4096]{1,0:T(8,128)(2,1)} fusion(bf16[256,4096]{1,0:T(8,128)(2,1)S(1)} %copy-done, bf16[384,4096]{1,0:T(8,128)(2,1)} %reshape.87, bf16[4096,256]{1,0:T(8,128)(2,1)} %param.22, f32[384,256]{1,0:T(8,128)S(1)} %fusion.34), kind=kOutput, calls=%fused_computation.1 | convolution fusion | flops 1612775424 | bytes 10878976 | tf_op jit(solution)/shard_map/dot_general | solution.py:101
  145.2 5.6 %reshape.88 = bf16[64,6,4096]{2,1,0:T(8,128)(2,1)} reshape(bf16[384,4096]{1,0:T(8,128)(2,1)} %convolution_convert_fusion) | data formatting | bytes 6291456 | tf_op jit(solution)/shard_map/reshape | solution.py:103
  150.9 6.8 %all-to-all-start.2 = ((bf16[64,6,4096]{2,1,0:T(8,128)(2,1)}), bf16[64,6,4096]{2,1,0:T(8,128)(2,1)}, u32[]{:S(2)}, u32[]{:S(2)}) async-start(bf16[64,6,4096]{2,1,0:T(8,128)(2,1)} %reshape.88), calls=%async_computation.2 | async-start | bytes 8388608 | tf_op jit(solution)/shard_map/all_to_all | solution.py:102
  159.9 28.8 %collective-permute-done.4 = bf16[16,4,4096]{2,1,0:T(4,128)(2,1)S(1)} collective-permute-done((bf16[16,4,4096]{2,1,0:T(4,128)(2,1)S(1)}, bf16[16,4,4096]{2,1,0:T(4,128)(2,1)S(1)}, u32[]{:S(2)}, u32[]{:S(2)}) %collective-permute-start.4) | collective-permute-done | bytes 524320 | tf_op jit(solution)/shard_map/ppermute | solution.py:24
  190.0 2.7 collective-permute-start.5
  192.7 42.6 %collective-permute-done.5 = bf16[32,4,4096]{2,1,0:T(4,128)(2,1)} collective-permute-done((bf16[32,4,4096]{2,1,0:T(4,128)(2,1)S(1)}, bf16[32,4,4096]{2,1,0:T(4,128)(2,1)}, u32[]{:S(2)}, u32[]{:S(2)}) %collective-permute-start.5) | collective-permute-done | bytes 1048608 | tf_op jit(solution)/shard_map/ppermute | solution.py:24
  235.3 2.8 pad_maximum_fusion
  240.5 4.1 %reshape_reshape.3 = bf16[256,4096]{1,0:T(8,128)(2,1)} reshape(bf16[2,32,4,4096]{3,2,1,0:T(4,128)(2,1)} %reverse_select_fusion) | data formatting | bytes 4194304 | tf_op jit(solution)/shard_map/reshape;reshape | solution.py:16
  246.8 4.8 %convolution_convert_fusion.1 = bf16[256,4096]{1,0:T(8,128)(2,1)} fusion(bf16[128,4096]{1,0:T(8,128)(2,1)} %param.20, bf16[256,4096]{1,0:T(8,128)(2,1)} %reshape_reshape.3, bf16[4096,128]{1,0:T(8,128)(2,1)} %param.19, f32[256,128]{1,0:T(8,128)S(1)} %fusion.33), kind=kOutput, calls=%fused_computation.2 | convolution fusion | flops 538116096 | bytes 6422528 | tf_op jit(solution)/shard_map/dot_general | solution.py:75
  251.6 4.1 %reshape.84 = bf16[64,4,4096]{2,1,0:T(4,128)(2,1)} reshape(bf16[256,4096]{1,0:T(8,128)(2,1)} %convolution_convert_fusion.1) | data formatting | bytes 4194304 | tf_op jit(solution)/shard_map/reshape | solution.py:33
  255.8 21.2 %all-to-all-start = ((bf16[64,4,4096]{2,1,0:T(4,128)(2,1)}), bf16[64,4,4096]{2,1,0:T(4,128)(2,1)}, u32[]{:S(2)}, u32[]{:S(2)}) async-start(bf16[64,4,4096]{2,1,0:T(4,128)(2,1)} %reshape.84), calls=%async_computation | async-start | bytes 4194304 | tf_op jit(solution)/shard_map/all_to_all | solution.py:39
  277.0 3.3 convert_reduce_fusion
  281.3 2.4 fusion.35
  283.6 44.5 %all-to-all-done = bf16[64,4,4096]{2,1,0:T(4,128)(2,1)} async-done(((bf16[64,4,4096]{2,1,0:T(4,128)(2,1)}), bf16[64,4,4096]{2,1,0:T(4,128)(2,1)}, u32[]{:S(2)}, u32[]{:S(2)}) %all-to-all-start) | async-done | bytes 2097184 | tf_op jit(solution)/shard_map/all_to_all | solution.py:39
  328.1 4.0 %all-to-all-start.3 = ((f32[4,4,4096]{2,1,0:T(4,128)}), f32[4,4,4096]{2,1,0:T(4,128)S(1)}, u32[]{:S(2)}, u32[]{:S(2)}) async-start(f32[4,4,4096]{2,1,0:T(4,128)} %fusion.35), calls=%async_computation.3 | async-start | bytes 524288 | tf_op jit(solution)/shard_map/all_to_all | solution.py:45
  332.1 2.4 convert_reduce_fusion.1
  334.6 3.3 all-to-all-done.3
  (47 shorter events, 19.2 us)
Async XLA Ops:
  0.0 137.6 %copy-start = (bf16[256,4096]{1,0:T(8,128)(2,1)S(1)}, bf16[256,4096]{1,0:T(8,128)(2,1)}, u32[]{:S(2)}) copy-start(bf16[256,4096]{1,0:T(8,128)(2,1)} %param.23) | copy-start | bytes 6291460
  7.8 13.5 %copy-start.2 = (bf16[4,4096]{1,0:T(4,128)(2,1)S(1)}, bf16[4,4096]{1,0:T(4,128)(2,1)}, u32[]{:S(2)}) copy-start(bf16[4,4096]{1,0:T(4,128)(2,1)} %param.12) | copy-start | bytes 98308
  7.8 13.6 %copy-start.3 = (f32[4096]{0:T(1024)S(1)}, f32[4096]{0:T(1024)}, u32[]{:S(2)}) copy-start(f32[4096]{0:T(1024)} %param.16) | copy-start | bytes 49156
  7.9 120.5 %all-to-all-start.1 = ((bf16[64,6,4096]{2,1,0:T(8,128)(2,1)}), bf16[64,6,4096]{2,1,0:T(8,128)(2,1)}, u32[]{:S(2)}, u32[]{:S(2)}) async-start(bf16[64,6,4096]{2,1,0:T(8,128)(2,1)} %bitcast.40), calls=%async_computation.1 | async-start | bytes 8388608 | tf_op jit(solution)/shard_map/all_to_all | solution.py:95
  21.6 1.5 collective-permute-start
  23.2 91.2 %collective-permute-start.1 = (bf16[2,4,4096]{2,1,0:T(4,128)(2,1)S(1)}, bf16[2,4,4096]{2,1,0:T(4,128)(2,1)S(1)}, u32[]{:S(2)}, u32[]{:S(2)}) collective-permute-start(bf16[2,4,4096]{2,1,0:T(4,128)(2,1)S(1)} %get-tuple-element.8), channel_id=1, source_target_pairs={{0,8},{4,12},{8,0},{12,4},{16,24},{20,28},{24,16},{28,20},{32,40},... | collective-permute-start | bytes 196616 | tf_op jit(solution)/shard_map/ppermute | solution.py:24
  114.5 9.2 %collective-permute-start.2 = (bf16[4,4,4096]{2,1,0:T(4,128)(2,1)S(1)}, bf16[4,4,4096]{2,1,0:T(4,128)(2,1)S(1)}, u32[]{:S(2)}, u32[]{:S(2)}) collective-permute-start(bf16[4,4,4096]{2,1,0:T(4,128)(2,1)S(1)} %bitcast.47), channel_id=1, source_target_pairs={{0,16},{4,20},{8,24},{12,28},{16,0},{20,4},{24,8},{28,12},{32,48},... | collective-permute-start | bytes 393224 | tf_op jit(solution)/shard_map/ppermute | solution.py:24
  124.0 33.6 %collective-permute-start.3 = (bf16[8,4,4096]{2,1,0:T(4,128)(2,1)S(1)}, bf16[8,4,4096]{2,1,0:T(4,128)(2,1)S(1)}, u32[]{:S(2)}, u32[]{:S(2)}) collective-permute-start(bf16[8,4,4096]{2,1,0:T(4,128)(2,1)S(1)} %bitcast.45), channel_id=1, source_target_pairs={{0,32},{4,36},{8,40},{12,44},{16,48},{20,52},{24,56},{28,60},{32,0... | collective-permute-start | bytes 786440 | tf_op jit(solution)/shard_map/ppermute | solution.py:24
  150.9 104.9 %all-to-all-start.2 = ((bf16[64,6,4096]{2,1,0:T(8,128)(2,1)}), bf16[64,6,4096]{2,1,0:T(8,128)(2,1)}, u32[]{:S(2)}, u32[]{:S(2)}) async-start(bf16[64,6,4096]{2,1,0:T(8,128)(2,1)} %reshape.88), calls=%async_computation.2 | async-start | bytes 8388608 | tf_op jit(solution)/shard_map/all_to_all | solution.py:102
  158.3 30.5 %collective-permute-start.4 = (bf16[16,4,4096]{2,1,0:T(4,128)(2,1)S(1)}, bf16[16,4,4096]{2,1,0:T(4,128)(2,1)S(1)}, u32[]{:S(2)}, u32[]{:S(2)}) collective-permute-start(bf16[16,4,4096]{2,1,0:T(4,128)(2,1)S(1)} %bitcast.43), channel_id=1, source_target_pairs={{0,64},{4,68},{8,72},{12,76},{16,80},{20,84},{24,88},{28,92},{32,9... | collective-permute-start | bytes 1572872 | tf_op jit(solution)/shard_map/ppermute | solution.py:24
  190.0 45.3 %collective-permute-start.5 = (bf16[32,4,4096]{2,1,0:T(4,128)(2,1)S(1)}, bf16[32,4,4096]{2,1,0:T(4,128)(2,1)}, u32[]{:S(2)}, u32[]{:S(2)}) collective-permute-start(bf16[32,4,4096]{2,1,0:T(4,128)(2,1)S(1)} %bitcast.41), channel_id=1, source_target_pairs={{0,128},{4,132},{8,136},{12,140},{16,144},{20,148},{24,152},{28,15... | collective-permute-start | bytes 3145736 | tf_op jit(solution)/shard_map/ppermute | solution.py:24
  240.5 4.1 %copy-start.1 = (bf16[4096,128]{1,0:T(8,128)(2,1)S(1)}, bf16[4096,128]{1,0:T(8,128)(2,1)}, u32[]{:S(2)}) copy-start(bf16[4096,128]{1,0:T(8,128)(2,1)} %param.18) | copy-start | bytes 3145732
  255.8 72.3 %all-to-all-start = ((bf16[64,4,4096]{2,1,0:T(4,128)(2,1)}), bf16[64,4,4096]{2,1,0:T(4,128)(2,1)}, u32[]{:S(2)}, u32[]{:S(2)}) async-start(bf16[64,4,4096]{2,1,0:T(4,128)(2,1)} %reshape.84), calls=%async_computation | async-start | bytes 4194304 | tf_op jit(solution)/shard_map/all_to_all | solution.py:39
  328.1 9.8 %all-to-all-start.3 = ((f32[4,4,4096]{2,1,0:T(4,128)}), f32[4,4,4096]{2,1,0:T(4,128)S(1)}, u32[]{:S(2)}, u32[]{:S(2)}) async-start(f32[4,4,4096]{2,1,0:T(4,128)} %fusion.35), calls=%async_computation.3 | async-start | bytes 524288 | tf_op jit(solution)/shard_map/all_to_all | solution.py:45
